TPU v7x, 32 devices: a whole 2x2x4 slice. The times are simulated.
32 devices in a mesh: dir: 4 (over z), bl: 8 (over y, x, core).
Axes of the slice: x: 2, y: 2, z: 4, core: 2. Of those that a mesh axis runs over, the one named last changes fastest.
Arguments:
- observed: float32 [32, 2, 30720], P('dir', None, 'bl'), may hold values from -6 to 6
- baseline_uvw_rows: float32 [3, 65536], P(None, 'bl'), may hold values from -600 to 600
- frequencies: float32 [32], replicated, may hold values from 0.8 to 1.2
- source_offset: float32 [2, 128], replicated, may hold values from -0.05 to 0.05
- source_flux: float32 [32, 128], replicated, may hold values from 0.02 to 0.3
- source_group: int32 [128], replicated, may hold values from 0 to 3, as said below
- direction_gain: float32 [4, 32, 2, 512], P('dir'), may hold values from -4.2 to 4.2
- station_first: int32 [4096], replicated, may hold values from 0 to 511
- station_second: int32 [4096], replicated, may hold values from 0 to 511
- average_exponent: int32 [4096], replicated, may hold values from 0 to 4, as said below
- owner_plan: int32 [8, 8], replicated, may hold values from 0 to 7, as said below
Outputs:
- residual: float32 [32, 2, 30720], P('dir', None, 'bl')
Inputs may be any that keep to these rules, and one draw needn't show every extreme that they name: `source_group`: each of the 4 groups is named by exactly 32 sources. `average_exponent`: summed over the blocks that owner_plan gives one owner, the averaged rows are at most 3840, and some owner has exactly 3840. Each row of owner_plan names every owner exactly once.
All inputs are finite; a program needn't handle non-finite values.
Results may differ from a plain program's by a relative error of at most 0.0003.
Values sent between devices are 32-bit elements; how exact they have to be, the bound alone decides.
A program may use at most 64 MiB of HBM per device.

v0:
```python
import functools
import math

import jax
import jax.numpy as jnp
from jax import lax
from jax.experimental import pallas as pl
from jax.experimental.pallas import tpu as pltpu
from jax.sharding import PartitionSpec as P

LANES = 128
UNROLL = 32
MESH = pl.DeviceIdType.MESH
HIGH = lax.Precision.HIGHEST
NT = (((1,), (1,)), ((), ()))
P0, P1, P2, P3 = -2.2636507847492298, 1.3870216243251186, 4.937789609959605, 0.5033641130059734
K0, K1, K2 = 0.9997897140197886, -10.245898871410082, 1.823099221649536


def iota(shape, axis):
    return lax.broadcasted_iota(jnp.int32, shape, axis)


def take(values, index):
    return jnp.take_along_axis(values, index, axis=1, mode="promise_in_bounds")


def prepare_kernel(
    groups,
    owners,
    time,
    uvw_ref,
    freq_ref,
    offs_ref,
    flux_ref,
    group_ref,
    gain_ref,
    ids_ref,
    exps_ref,
    plan_ref,
    plan_smem,
    sky_ref,
    wide_ref,
    base_ref,
    order_ref,
    pair_ref,
    mask_ref,
    start_ref,
    table_ref,
):
    d = lax.axis_index("dir")
    p = lax.axis_index("bl")
    cl = wide_ref.shape[1]
    sources = offs_ref.shape[1]
    per_group = sources // groups
    bl_dev = ids_ref.shape[1]
    block_len = bl_dev // owners
    slots = block_len * time
    block_tiles = slots // LANES
    per_tile = LANES // time
    log_time = int(math.log2(time))
    chunks = bl_dev // LANES

    for k in range(owners):
        order_ref[plan_smem[p, k]] = uvw_ref[:, k * slots : (k + 1) * slots]
    plan = plan_ref[...].astype(jnp.float32)
    own_plan = jnp.sum(
        jnp.where(iota((owners, owners), 0) == p, plan, 0.0), axis=0, keepdims=True
    )
    held_by = jnp.abs(own_plan - iota((owners, owners), 0).astype(jnp.float32)) < 0.5
    block_of = jnp.sum(
        jnp.where(held_by, iota((owners, owners), 1).astype(jnp.float32), 0.0), axis=1, keepdims=True
    )

    member_row = group_ref[...].astype(jnp.float32)
    eye = (iota((sources, sources), 0) == iota((sources, sources), 1)).astype(jnp.float32)
    member_col = lax.dot_general(eye, member_row, NT, precision=HIGH)
    earlier = iota((sources, sources), 0) < iota((sources, sources), 1)
    same = (jnp.abs(member_col - member_row) < 0.5) & earlier
    rank = jnp.sum(same.astype(jnp.float32), axis=0, keepdims=True)
    place = (member_row * per_group + rank + 0.5).astype(jnp.int32)
    pick = (iota((sources, sources), 0) == place).astype(jnp.float32)
    offs = lax.dot_general(pick, offs_ref[...], NT, precision=HIGH)
    east, north = offs[:, 0:1], offs[:, 1:2]
    depth = jnp.sqrt(1.0 - east * east - north * north) - 1.0
    sky_ref[0] = jnp.broadcast_to(east, sky_ref.shape[1:])
    sky_ref[1] = jnp.broadcast_to(north, sky_ref.shape[1:])
    sky_ref[2] = jnp.broadcast_to(depth, sky_ref.shape[1:])
    channel = iota((cl, flux_ref.shape[0]), 1) == d * cl + iota((cl, flux_ref.shape[0]), 0)
    channel = channel.astype(jnp.float32)
    own_flux = jnp.dot(channel, flux_ref[...], precision=HIGH)
    flux = lax.dot_general(own_flux, pick, NT, precision=HIGH)
    for k in range(sources):
        wide_ref[k] = jnp.broadcast_to(flux[:, k : k + 1], (cl, LANES))
    for g in range(groups):
        part = jnp.sum(flux[:, g * per_group : (g + 1) * per_group], axis=1, keepdims=True)
        base_ref[g] = jnp.broadcast_to(part, (cl, LANES))
    freq = jnp.sum(channel * freq_ref[...], axis=1, keepdims=True)
    base_ref[groups] = jnp.broadcast_to(freq, (cl, LANES))

    lane = iota((owners, LANES), 1)
    row = iota((owners, LANES), 0)
    station_total = gain_ref.shape[3]
    for g in range(groups):
        for z in range(2):
            table_ref[g, z] = gain_ref[0, g * cl : (g + 1) * cl, z, :]
    for chunk in range(chunks):
        lanes = pl.ds(chunk * LANES, LANES)
        where_from = jnp.where((chunk * LANES + lane) // block_len == row, block_of, 0.0)
        where_from = (jnp.sum(where_from, axis=0, keepdims=True) + 0.5).astype(jnp.int32)
        source = where_from * block_len + (chunk * LANES + iota((1, LANES), 1)) % block_len
        source = jnp.broadcast_to(source, (cl, LANES))
        looked = []
        for which in range(2):
            ids = jnp.zeros((cl, LANES), jnp.int32)
            for part in range(chunks):
                table = ids_ref[which : which + 1, part * LANES : (part + 1) * LANES]
                table = jnp.broadcast_to(table, (cl, LANES))
                ids = jnp.where((source >> 7) == part, take(table, source & (LANES - 1)), ids)
            low, high = ids & (LANES - 1), ids >> 7
            rows = []
            for g in range(groups):
                for z in range(2):
                    total = jnp.zeros((cl, LANES), jnp.float32)
                    for part in range(station_total // LANES):
                        table = table_ref[g, z, :, pl.ds(part * LANES, LANES)]
                        total = jnp.where(high == part, take(table, low), total)
                    rows.append(total)
            looked.append(rows)
        first, second = looked
        for g in range(groups):
            ar, ai, br, bi = first[2 * g], first[2 * g + 1], second[2 * g], second[2 * g + 1]
            pair_ref[g, 0, :, lanes] = ar * br + ai * bi
            pair_ref[g, 1, :, lanes] = ai * br - ar * bi

    rows_all = jnp.right_shift(jnp.full(exps_ref.shape, time, jnp.int32), exps_ref[...])
    rows_all = rows_all.astype(jnp.float32)
    to_owner = jnp.zeros((owners, 1), jnp.float32)
    for k in range(owners):
        count = jnp.sum(rows_all[:, k * block_len : (k + 1) * block_len], axis=1, keepdims=True)
        to_owner = to_owner + jnp.where(plan_ref[:, k : k + 1] == p, count, 0.0)
    starts = jnp.sum(jnp.where(row < lane, to_owner, 0.0), axis=0, keepdims=True)
    start_ref[...] = (starts + 0.5).astype(jnp.int32)

    exps = []
    for t in range(block_tiles):
        source = (block_of + 0.5).astype(jnp.int32) * block_len + t * per_tile + lane // time
        found = jnp.zeros((owners, LANES), jnp.int32)
        for part in range(chunks):
            table = ids_ref[2:3, part * LANES : (part + 1) * LANES]
            table = jnp.broadcast_to(table, (owners, LANES))
            if owners > 8:
                got = jnp.concatenate(
                    [take(table[i : i + 8], source[i : i + 8] & (LANES - 1)) for i in range(0, owners, 8)]
                )
            else:
                got = take(table, source & (LANES - 1))
            found = jnp.where((source >> 7) == part, got, found)
        exps.append(found)
    exps = jnp.concatenate(exps, axis=1)

    def put(index, values):
        for t in range(block_tiles):
            mask_ref[index, t] = values[:, t * LANES : (t + 1) * LANES]

    position = iota((owners, slots), 1)
    width = jnp.left_shift(jnp.ones_like(exps), exps)
    valid = ((position & (width - 1)) == 0).astype(jnp.int32)
    prefix = valid
    shift = 1
    while shift < slots:
        prefix = prefix + jnp.where(position >= shift, pltpu.roll(prefix, shift, 1), 0)
        shift *= 2
    count = jnp.max(prefix, axis=1, keepdims=True)
    move = position - (prefix - valid)
    scale = jnp.ones((owners, slots), jnp.float32)
    for s in range(log_time):
        scale = jnp.where(exps > s, scale * 0.5, scale)
        put(s, (exps > s).astype(jnp.float32))
    bits = int(math.log2(slots))
    held = jnp.where(valid == 1, move, 0)
    for b in range(bits):
        here = (held >> b) & 1
        moved = pltpu.roll(held, slots - (1 << b), 1)
        come = (moved >> b) & 1
        put(log_time + b, come.astype(jnp.float32))
        held = jnp.where(come == 1, moved, jnp.where(here == 1, 0, held))
    put(log_time + bits, (position < count).astype(jnp.float32))
    put(log_time + bits + 1, scale)


def predict_kernel(
    groups,
    owners,
    time,
    tiles,
    sky_ref,
    wide_ref,
    base_ref,
    order_ref,
    pair_ref,
    mask_ref,
    piece_ref,
    q_ref,
    sum_ref,
    send_ref,
    gather_ref,
    gain_send,
    gain_recv,
    piece_send,
    piece_recv,
):
    d = lax.axis_index("dir")
    p = lax.axis_index("bl")
    sources, cl, _ = wide_ref.shape
    per_group = sources // groups
    slots = order_ref.shape[2]
    block_len = slots // time
    block_tiles = slots // LANES
    per_tile = LANES // time
    log_time = int(math.log2(time))
    bits = int(math.log2(slots))

    barrier = pltpu.get_barrier_semaphore()
    for axis, me, size in (("dir", d, groups), ("bl", p, owners)):
        for step in range(1, size):
            pl.semaphore_signal(
                barrier, inc=1, device_id={axis: lax.rem(me + step, size)}, device_id_type=MESH
            )

    def gain_copy(step):
        other = lax.rem(d + step, groups)
        return pltpu.make_async_remote_copy(
            src_ref=pair_ref.at[other],
            dst_ref=gather_ref.at[d],
            send_sem=gain_send.at[step - 1],
            recv_sem=gain_recv.at[step - 1],
            device_id={"dir": other},
            device_id_type=MESH,
        )

    def piece_copy(step):
        return pltpu.make_async_remote_copy(
            src_ref=send_ref.at[step],
            dst_ref=piece_ref.at[p],
            send_sem=piece_send.at[step],
            recv_sem=piece_recv.at[step],
            device_id={"bl": lax.rem(p + 1 + step, owners)},
            device_id_type=MESH,
        )

    gather_ref[d] = pair_ref[d]
    pl.semaphore_wait(barrier, groups - 1 + owners - 1)
    for step in range(1, groups):
        gain_copy(step).start()
    freq = base_ref[groups]
    flux_sum = [base_ref[g] for g in range(groups)]
    lane = iota((cl, LANES), 1)

    def block_body(turn, carry):
        owner = lax.rem(p + 1 + turn, owners)
        for t in range(block_tiles):
            ln = slice(t * LANES, (t + 1) * LANES)
            u = order_ref[owner, 0:1, ln]
            v = order_ref[owner, 1:2, ln]
            w = order_ref[owner, 2:3, ln]
            q_ref[t] = sky_ref[0] * u + sky_ref[1] * v + sky_ref[2] * w

        @pl.when(turn > 0)
        def _():
            piece_copy(turn - 1).start()

        def tile_body(step, carry):
            for g in range(groups):

                def source(i, acc):
                    acc = list(acc)
                    index = g * per_group + i
                    amount = wide_ref[index]
                    for t in range(tiles):
                        turns = freq * q_ref[step * tiles + t, pl.ds(index, cl, stride=0), :]
                        x = turns - jnp.round(turns)
                        z = x * x
                        m = (z + P0) * z
                        s = x * (m + P1)
                        weighted = amount * s
                        acc[2 * t] = acc[2 * t] + weighted * s
                        acc[2 * t + 1] = acc[2 * t + 1] + weighted * ((m + P2) * (m + P3))
                    return tuple(acc)

                acc = tuple(jnp.zeros((cl, LANES), jnp.float32) for _ in range(2 * tiles))
                acc = lax.fori_loop(0, per_group, source, acc, unroll=UNROLL)
                for t in range(tiles):
                    sum_ref[step * tiles + t, 2 * g] = K0 * flux_sum[g] + K1 * acc[2 * t]
                    sum_ref[step * tiles + t, 2 * g + 1] = -K2 * acc[2 * t + 1]
            return carry

        lax.fori_loop(0, block_tiles // tiles, tile_body, 0)

        @pl.when(turn == 0)
        def _():
            for step in range(1, groups):
                gain_copy(step).wait()

        model = ([], [])
        for t in range(block_tiles):
            first_bl = owner * block_len + t * per_tile
            chunk = pl.multiple_of((first_bl // LANES) * LANES, LANES)
            index = first_bl % LANES + lane // time
            model_r = jnp.zeros((cl, LANES), jnp.float32)
            model_i = jnp.zeros((cl, LANES), jnp.float32)
            for g in range(groups):
                gr = take(gather_ref[g, 0, :, pl.ds(chunk, LANES)], index)
                gi = take(gather_ref[g, 1, :, pl.ds(chunk, LANES)], index)
                real, imag = sum_ref[t, 2 * g], sum_ref[t, 2 * g + 1]
                model_r = model_r + (real * gr - imag * gi)
                model_i = model_i + (real * gi + imag * gr)
            model[0].append(model_r)
            model[1].append(model_i)

        def wide(index):
            return jnp.concatenate(
                [mask_ref[index, t, pl.ds(owner, cl, stride=0), :] for t in range(block_tiles)], axis=1
            )

        for z in range(2):
            x = jnp.concatenate(model[z], axis=1) * wide(log_time + bits + 1)
            for s in range(log_time):
                x = x + wide(s) * pltpu.roll(x, slots - (1 << s), 1)
            for b in range(bits):
                x = jnp.where(wide(log_time + b) > 0.5, pltpu.roll(x, slots - (1 << b), 1), x)
            send_ref[turn, z] = jnp.where(wide(log_time + bits) > 0.5, x, 0.0)
        return carry

    lax.fori_loop(0, owners, block_body, 0)
    piece_ref[p] = send_ref[owners - 1]
    for step in range(owners - 1):
        piece_copy(step).wait()


def place_kernel(start_ref, piece_ref, observed_ref, out_ref, total_ref):
    owners, _, cl, slots = piece_ref.shape
    capacity = observed_ref.shape[2]
    total_ref[...] = jnp.zeros_like(total_ref)
    position = iota((cl, LANES), 1)
    for index in range(owners):
        start = start_ref[0, index]
        low = start & (LANES - 1)
        base = pl.multiple_of(start - low, LANES)
        for z in range(2):
            spun = [
                pltpu.roll(piece_ref[index, z, :, pl.ds(t * LANES, LANES)], low, 1)
                for t in range(slots // LANES)
            ]
            for t in range(slots // LANES + 1):
                value = jnp.zeros((cl, LANES), jnp.float32)
                if t < slots // LANES:
                    value = jnp.where(position >= low, spun[t], value)
                if t > 0:
                    value = jnp.where(position < low, spun[t - 1], value)
                lanes = pl.ds(base + t * LANES, LANES)
                total_ref[z, :, lanes] = total_ref[z, :, lanes] + value
    for z in range(2):
        out_ref[:, z, :] = observed_ref[:, z, :] - total_ref[z, :, pl.ds(0, capacity)]


def on_device(
    observed,
    baseline_uvw_rows,
    frequencies,
    source_offset,
    source_flux,
    source_group,
    direction_gain,
    station_first,
    station_second,
    average_exponent,
    owner_plan,
):
    owners = lax.axis_size("bl")
    groups = lax.axis_size("dir")
    cl, _, capacity = observed.shape
    bl_dev = station_first.shape[0] // owners
    rows = baseline_uvw_rows.shape[1]
    time = rows // bl_dev
    slots = rows // owners
    tiles = slots // LANES
    sources = source_group.shape[0]
    ids = jnp.stack([station_first, station_second, average_exponent])
    ids = lax.dynamic_slice_in_dim(ids, lax.axis_index("bl") * bl_dev, bl_dev, 1)
    vmem = pl.BlockSpec(memory_space=pltpu.VMEM)
    smem = pl.BlockSpec(memory_space=pltpu.SMEM)
    masks = int(math.log2(time)) + int(math.log2(slots)) + 2
    f32 = jnp.float32
    shape = jax.ShapeDtypeStruct
    *prepared, starts = pl.pallas_call(
        functools.partial(prepare_kernel, groups, owners, time),
        out_shape=(
            shape((3, sources, LANES), f32),
            shape((sources, cl, LANES), f32),
            shape((groups + 1, cl, LANES), f32),
            shape((owners, 3, slots), f32),
            shape((groups, 2, cl, bl_dev), f32),
            shape((masks, tiles, owners, LANES), f32),
            shape((1, LANES), jnp.int32),
        ),
        in_specs=[vmem] * 9 + [smem],
        out_specs=(vmem,) * 7,
        scratch_shapes=[pltpu.VMEM((groups, 2, cl, direction_gain.shape[3]), f32)],
        compiler_params=pltpu.CompilerParams(vmem_limit_bytes=32 << 20),
        name="prepare",
    )(
        baseline_uvw_rows,
        frequencies.reshape(1, -1),
        source_offset,
        source_flux,
        source_group.reshape(1, -1),
        direction_gain,
        ids,
        average_exponent.reshape(owners, bl_dev),
        owner_plan,
        owner_plan,
    )
    dma = pltpu.SemaphoreType.DMA
    pieces = pl.pallas_call(
        functools.partial(predict_kernel, groups, owners, time, min(4, tiles)),
        out_shape=shape((owners, 2, cl, slots), f32),
        in_specs=[vmem] * 6,
        out_specs=vmem,
        scratch_shapes=[
            pltpu.VMEM((tiles, sources, LANES), f32),
            pltpu.VMEM((tiles, 2 * groups, cl, LANES), f32),
            pltpu.VMEM((owners, 2, cl, slots), f32),
            pltpu.VMEM((groups, 2, cl, bl_dev), f32),
            dma((groups - 1,)),
            dma((groups - 1,)),
            dma((owners - 1,)),
            dma((owners - 1,)),
        ],
        compiler_params=pltpu.CompilerParams(
            vmem_limit_bytes=32 << 20, collective_id=0, has_side_effects=True
        ),
        name="predict",
    )(*prepared)
    return pl.pallas_call(
        place_kernel,
        out_shape=jax.ShapeDtypeStruct(observed.shape, f32),
        in_specs=[smem, vmem, vmem],
        out_specs=vmem,
        scratch_shapes=[pltpu.VMEM((2, cl, capacity + slots + LANES), f32)],
        compiler_params=pltpu.CompilerParams(vmem_limit_bytes=32 << 20),
        name="place",
    )(starts, pieces, observed)


def solution(mesh):
    placed = (
        P("dir", None, "bl"),
        P(None, "bl"),
        P(),
        P(),
        P(),
        P(),
        P("dir", None, None, None),
        P(),
        P(),
        P(),
        P(),
    )
    return jax.shard_map(
        on_device, mesh=mesh, in_specs=placed, out_specs=P("dir", None, "bl"), check_vma=False
    )
```

profile of v0, /device:TPU:0, one launch (start us, length us, event | category | flops | bytes accessed | tf_op | source)
XLA Modules:
  0.0 43.2 jit_solution(7242505590818733594)
XLA Ops:
  0.0 0.0 copy-start.8
  0.0 0.7 %copy-done.8 = s32[4096]{0:T(1024)S(1)} copy-done((s32[4096]{0:T(1024)S(1)}, s32[4096]{0:T(1024)}, u32[]{:S(2)}) %copy-start.8) | copy-done | bytes 16408
  0.7 0.8 %fusion.1.ids_ref = s32[3,512]{1,0:T(4,128)S(1)} fusion(s32[]{:T(128)S(6)} %select_n.3, s32[1,4096]{1,0:T(1,128)S(1)} %bitcast.7, s32[1,4096]{1,0:T(1,128)} %bitcast.8, s32[1,4096]{1,0:T(1,128)} %bitcast.9), kind=kLoop, calls=%fused_computation.4 | loop fusion | flops 3072 | bytes 55300 | tf_op jit(solution)/shard_map/stack | solution.py:389
  1.5 0.0 copy-start.3
  1.5 0.0 copy-start.4
  1.5 0.0 copy-start.5
  1.5 0.0 copy-start.6
  1.5 0.0 copy-start.7
  1.6 0.6 %copy-done.3 = s32[8,8]{1,0:T(8,128)S(1)} copy-done((s32[8,8]{1,0:T(8,128)S(1)}, s32[8,8]{1,0:T(8,128)}, u32[]{:S(2)}) %copy-start.3) | copy-done | bytes 280
  2.2 0.0 copy-done.4
  2.2 0.0 copy-done.5
  2.2 0.0 copy-done.6
  2.2 0.0 copy-done.7
  2.2 0.0 copy-start.1
  2.2 0.9 %copy-done.1 = f32[3,8192]{1,0:T(4,128)S(1)} copy-done((f32[3,8192]{1,0:T(4,128)S(1)}, f32[3,8192]{1,0:T(4,128)}, u32[]{:S(2)}) %copy-start.1) | copy-done | bytes 98328
  3.1 0.0 copy-start.2
  3.1 0.9 %copy-done.2 = f32[1,32,2,512]{3,2,1,0:T(2,128)S(1)} copy-done((f32[1,32,2,512]{3,2,1,0:T(2,128)S(1)}, f32[1,32,2,512]{3,2,1,0:T(2,128)}, u32[]{:S(2)}) %copy-start.2) | copy-done | bytes 131096
  4.1 2.9 %prepare.1 = (f32[3,128,128]{2,1,0:T(8,128)S(1)}, f32[128,8,128]{2,1,0:T(8,128)S(1)}, f32[5,8,128]{2,1,0:T(8,128)S(1)}, f32[8,3,1024]{2,1,0:T(4,128)S(1)}, f32[4...) custom-call(f32[3,8192]{1,0:T(4,128)S(1)} %copy-done.1, f32[1,32]{1,0:T(1,128)S(1)} %bitcast.5, ...), custom_call_target="tpu_custom_call" | custom-call | tf_op jit(solution)/shard_map/prepare/pallas_call | solution.py:396
  6.9 0.0 copy-start
  6.9 34.4 %predict.1.piece_ref = f32[8,2,8,1024]{3,2,1,0:T(8,128)S(1)} custom-call(f32[3,128,128]{2,1,0:T(8,128)S(1)} %get-tuple-element.13.sky_ref, f32[128,8,128]{2,1,0:T(8,128)S(1)} %get-tuple-element.14.wide_ref, f32[5,8,128]{2,1,0:T(8,128)S(1)} %get-tuple-element.15.base_ref, f32[8,3,1024]{2,1,0:T(4,128)S(1)} %get-tuple-element.16.order_ref, ...), custom_call_target="tpu_custom_call" | custom-call | tf_op jit(solution)/shard_map/predict/pallas_call | solution.py:425
  41.4 0.0 copy-done
  41.4 1.8 %place.1 = f32[8,2,3840]{2,1,0:T(2,128)} custom-call(s32[1,128]{1,0:T(1,128)S(1)} %get-tuple-element.12.start_ref, f32[8,2,8,1024]{3,2,1,0:T(8,128)S(1)} %predict.1.piece_ref, f32[8,2,3840]{2,1,0:T(2,128)S(1)} %copy-done), custom_call_target="tpu_custom_call" | custom-call | tf_op jit(solution)/shard_map/place/pallas_call | solution.py:445
  (1 shorter events, 0.0 us)
Async XLA Ops:
  0.0 0.7 %copy-start.8 = (s32[4096]{0:T(1024)S(1)}, s32[4096]{0:T(1024)}, u32[]{:S(2)}) copy-start(s32[4096]{0:T(1024)} %param.20) | copy-start | bytes 49156
  1.5 0.7 %copy-start.3 = (s32[8,8]{1,0:T(8,128)S(1)}, s32[8,8]{1,0:T(8,128)}, u32[]{:S(2)}) copy-start(s32[8,8]{1,0:T(8,128)} %plan_smem.1) | copy-start | bytes 772
  1.5 0.7 %copy-start.4 = (f32[32,128]{1,0:T(8,128)S(1)}, f32[32,128]{1,0:T(8,128)}, u32[]{:S(2)}) copy-start(f32[32,128]{1,0:T(8,128)} %flux_ref.1) | copy-start | bytes 49156
  1.5 0.7 %copy-start.5 = (f32[2,128]{1,0:T(2,128)S(1)}, f32[2,128]{1,0:T(2,128)}, u32[]{:S(2)}) copy-start(f32[2,128]{1,0:T(2,128)} %offs_ref.1) | copy-start | bytes 3076
  1.5 0.7 %copy-start.6 = (f32[32]{0:T(128)S(1)}, f32[32]{0:T(128)}, u32[]{:S(2)}) copy-start(f32[32]{0:T(128)} %param.13) | copy-start | bytes 388
  1.5 0.7 %copy-start.7 = (s32[128]{0:T(128)S(1)}, s32[128]{0:T(128)}, u32[]{:S(2)}) copy-start(s32[128]{0:T(128)} %param.16) | copy-start | bytes 1540
  2.2 0.9 %copy-start.1 = (f32[3,8192]{1,0:T(4,128)S(1)}, f32[3,8192]{1,0:T(4,128)}, u32[]{:S(2)}) copy-start(f32[3,8192]{1,0:T(4,128)} %uvw_ref.1) | copy-start | bytes 294916
  3.1 0.9 %copy-start.2 = (f32[1,32,2,512]{3,2,1,0:T(2,128)S(1)}, f32[1,32,2,512]{3,2,1,0:T(2,128)}, u32[]{:S(2)}) copy-start(f32[1,32,2,512]{3,2,1,0:T(2,128)} %gain_ref.1) | copy-start | bytes 393220
  6.9 34.4 %copy-start = (f32[8,2,3840]{2,1,0:T(2,128)S(1)}, f32[8,2,3840]{2,1,0:T(2,128)}, u32[]{:S(2)}) copy-start(f32[8,2,3840]{2,1,0:T(2,128)} %observed_ref.1) | copy-start | bytes 737284
where the time goes:
time: 43.5 us; the launch traced here: 43.2 us
  Pallas kernels  39.1 us (90%)
  local copies, waits for them, and re-layouts  3.23 us (7%)
  other arithmetic  0.78 us (2%)
    pallas_call x1, Pallas kernels, on_device(): pl.pallas_call(functools.partial(predict_kernel, groups, owners, time, mi...  34.4 us
    unnamed x18, local copies, waits for them, and re-layouts  3.23 us
    pallas_call x1, Pallas kernels, on_device(): pl.pallas_call(functools.partial(prepare_kernel, groups, owners, time), o...  2.86 us
    pallas_call x1, Pallas kernels, on_device(): pl.pallas_call(place_kernel, out_shape=jax.ShapeDtypeStruct(observed.shap...  1.84 us

commit v1 on v0

--- a/solution.py
+++ b/solution.py
@@ -203,6 +203,7 @@
     piece_ref,
     q_ref,
     sum_ref,
+    early_ref,
     send_ref,
     gather_ref,
     gain_send,
@@ -250,58 +251,46 @@
         )
 
     gather_ref[d] = pair_ref[d]
-    pl.semaphore_wait(barrier, groups - 1 + owners - 1)
-    for step in range(1, groups):
-        gain_copy(step).start()
     freq = base_ref[groups]
     flux_sum = [base_ref[g] for g in range(groups)]
     lane = iota((cl, LANES), 1)
-
-    def block_body(turn, carry):
-        owner = lax.rem(p + 1 + turn, owners)
-        for t in range(block_tiles):
-            ln = slice(t * LANES, (t + 1) * LANES)
+    steps = block_tiles // tiles
+
+    def owner_of(turn):
+        return lax.rem(p + 1 + turn, owners)
+
+    def add_sources(owner, step, keep_ref):
+        for t in range(tiles):
+            ln = pl.ds(pl.multiple_of((step * tiles + t) * LANES, LANES), LANES)
             u = order_ref[owner, 0:1, ln]
             v = order_ref[owner, 1:2, ln]
             w = order_ref[owner, 2:3, ln]
             q_ref[t] = sky_ref[0] * u + sky_ref[1] * v + sky_ref[2] * w
-
-        @pl.when(turn > 0)
-        def _():
-            piece_copy(turn - 1).start()
-
-        def tile_body(step, carry):
-            for g in range(groups):
-
-                def source(i, acc):
-                    acc = list(acc)
-                    index = g * per_group + i
-                    amount = wide_ref[index]
-                    for t in range(tiles):
-                        turns = freq * q_ref[step * tiles + t, pl.ds(index, cl, stride=0), :]
-                        x = turns - jnp.round(turns)
-                        z = x * x
-                        m = (z + P0) * z
-                        s = x * (m + P1)
-                        weighted = amount * s
-                        acc[2 * t] = acc[2 * t] + weighted * s
-                        acc[2 * t + 1] = acc[2 * t + 1] + weighted * ((m + P2) * (m + P3))
-                    return tuple(acc)
-
-                acc = tuple(jnp.zeros((cl, LANES), jnp.float32) for _ in range(2 * tiles))
-                acc = lax.fori_loop(0, per_group, source, acc, unroll=UNROLL)
+        for g in range(groups):
+
+            def source(i, acc):
+                acc = list(acc)
+                index = g * per_group + i
+                amount = wide_ref[index]
                 for t in range(tiles):
-                    sum_ref[step * tiles + t, 2 * g] = K0 * flux_sum[g] + K1 * acc[2 * t]
-                    sum_ref[step * tiles + t, 2 * g + 1] = -K2 * acc[2 * t + 1]
-            return carry
-
-        lax.fori_loop(0, block_tiles // tiles, tile_body, 0)
-
-        @pl.when(turn == 0)
-        def _():
-            for step in range(1, groups):
-                gain_copy(step).wait()
-
+                    turns = freq * q_ref[t, pl.ds(index, cl, stride=0), :]
+                    x = turns - jnp.round(turns)
+                    z = x * x
+                    m = (z + P0) * z
+                    s = x * (m + P1)
+                    weighted = amount * s
+                    acc[2 * t] = acc[2 * t] + weighted * s
+                    acc[2 * t + 1] = acc[2 * t + 1] + weighted * ((m + P2) * (m + P3))
+                return tuple(acc)
+
+            acc = tuple(jnp.zeros((cl, LANES), jnp.float32) for _ in range(2 * tiles))
+            acc = lax.fori_loop(0, per_group, source, acc, unroll=UNROLL)
+            for t in range(tiles):
+                keep_ref[step * tiles + t, 2 * g] = K0 * flux_sum[g] + K1 * acc[2 * t]
+                keep_ref[step * tiles + t, 2 * g + 1] = -K2 * acc[2 * t + 1]
+
+    def finish(turn, keep_ref):
+        owner = owner_of(turn)
         model = ([], [])
         for t in range(block_tiles):
             first_bl = owner * block_len + t * per_tile
@@ -312,7 +301,7 @@
             for g in range(groups):
                 gr = take(gather_ref[g, 0, :, pl.ds(chunk, LANES)], index)
                 gi = take(gather_ref[g, 1, :, pl.ds(chunk, LANES)], index)
-                real, imag = sum_ref[t, 2 * g], sum_ref[t, 2 * g + 1]
+                real, imag = keep_ref[t, 2 * g], keep_ref[t, 2 * g + 1]
                 model_r = model_r + (real * gr - imag * gi)
                 model_i = model_i + (real * gi + imag * gr)
             model[0].append(model_r)
@@ -323,17 +312,57 @@
                 [mask_ref[index, t, pl.ds(owner, cl, stride=0), :] for t in range(block_tiles)], axis=1
             )
 
+        scale = wide(log_time + bits + 1)
+        both = [jnp.concatenate(model[z], axis=1) * scale for z in range(2)]
+        for s in range(log_time):
+            mask = wide(s)
+            both = [x + mask * pltpu.roll(x, slots - (1 << s), 1) for x in both]
+        for b in range(bits):
+            mask = wide(log_time + b) > 0.5
+            both = [jnp.where(mask, pltpu.roll(x, slots - (1 << b), 1), x) for x in both]
+        mask = wide(log_time + bits) > 0.5
+        return [jnp.where(mask, x, 0.0) for x in both]
+
+    def send(turn, done):
         for z in range(2):
-            x = jnp.concatenate(model[z], axis=1) * wide(log_time + bits + 1)
-            for s in range(log_time):
-                x = x + wide(s) * pltpu.roll(x, slots - (1 << s), 1)
-            for b in range(bits):
-                x = jnp.where(wide(log_time + b) > 0.5, pltpu.roll(x, slots - (1 << b), 1), x)
-            send_ref[turn, z] = jnp.where(wide(log_time + bits) > 0.5, x, 0.0)
+            send_ref[turn, z] = done[z]
+
+    def early(index, carry):
+        turn = index // steps
+
+        @pl.when(index == steps)
+        def _():
+            pl.semaphore_wait(barrier, groups - 1 + owners - 1)
+            for step in range(1, groups):
+                gain_copy(step).start()
+
+        add_sources(owner_of(turn), lax.rem(index, steps), early_ref.at[turn])
         return carry
 
-    lax.fori_loop(0, owners, block_body, 0)
-    piece_ref[p] = send_ref[owners - 1]
+    lax.fori_loop(0, 2 * steps, early, 0)
+    for step in range(1, groups):
+        gain_copy(step).wait()
+    for step in range(steps):
+        done = [turn for turn in range(2) if min(turn, steps - 1) == step]
+        for turn in done:
+            send(turn, finish(turn, early_ref.at[turn]))
+        add_sources(owner_of(2), step, sum_ref)
+        for turn in done:
+            piece_copy(turn).start()
+
+    def block_body(turn, carry):
+        for step in range(steps):
+            if step == 0:
+                send(turn - 1, finish(turn - 1, sum_ref))
+            add_sources(owner_of(turn), step, sum_ref)
+            if step == 0:
+                piece_copy(turn - 1).start()
+        return carry
+
+    lax.fori_loop(3, owners, block_body, 0)
+    done = finish(owners - 1, sum_ref)
+    for z in range(2):
+        piece_ref[p, z] = done[z]
     for step in range(owners - 1):
         piece_copy(step).wait()
 
@@ -353,13 +382,14 @@
                 for t in range(slots // LANES)
             ]
             for t in range(slots // LANES + 1):
-                value = jnp.zeros((cl, LANES), jnp.float32)
-                if t < slots // LANES:
-                    value = jnp.where(position >= low, spun[t], value)
-                if t > 0:
-                    value = jnp.where(position < low, spun[t - 1], value)
-                lanes = pl.ds(base + t * LANES, LANES)
-                total_ref[z, :, lanes] = total_ref[z, :, lanes] + value
+                lanes = pl.ds(pl.multiple_of(base + t * LANES, LANES), LANES)
+                if t == 0:
+                    value = jnp.where(position >= low, spun[t], total_ref[z, :, lanes])
+                elif t < slots // LANES:
+                    value = jnp.where(position >= low, spun[t], spun[t - 1])
+                else:
+                    value = jnp.where(position >= low, 0.0, spun[t - 1])
+                total_ref[z, :, lanes] = value
     for z in range(2):
         out_ref[:, z, :] = observed_ref[:, z, :] - total_ref[z, :, pl.ds(0, capacity)]
 
@@ -428,9 +458,10 @@
         in_specs=[vmem] * 6,
         out_specs=vmem,
         scratch_shapes=[
-            pltpu.VMEM((tiles, sources, LANES), f32),
+            pltpu.VMEM((min(4, tiles), sources, LANES), f32),
             pltpu.VMEM((tiles, 2 * groups, cl, LANES), f32),
-            pltpu.VMEM((owners, 2, cl, slots), f32),
+            pltpu.VMEM((2, tiles, 2 * groups, cl, LANES), f32),
+            pltpu.VMEM((owners - 1, 2, cl, slots), f32),
             pltpu.VMEM((groups, 2, cl, bl_dev), f32),
             dma((groups - 1,)),
             dma((groups - 1,)),

time: 43.5 us -> 39.6 us (0.910)
  the two profiles are of different devices: /device:TPU:0 before, /device:TPU:1 now
where the time goes in v1:
time: 39.6 us; the launch traced here: 39.3 us
  Pallas kernels  35.2 us (89%)
  local copies, waits for them, and re-layouts  3.23 us (8%)
  other arithmetic  0.78 us (2%)
    pallas_call x1, Pallas kernels, on_device(): pl.pallas_call(functools.partial(predict_kernel, groups, owners, time, mi...  30.8 us
    unnamed x18, local copies, waits for them, and re-layouts  3.23 us
    pallas_call x1, Pallas kernels, on_device(): pl.pallas_call(functools.partial(prepare_kernel, groups, owners, time), o...  2.86 us
    pallas_call x1, Pallas kernels, on_device(): pl.pallas_call(place_kernel, out_shape=jax.ShapeDtypeStruct(observed.shap...  1.51 us

profile of v1, /device:TPU:1, one launch (start us, length us, event | category | flops | bytes accessed | tf_op | source)
XLA Modules:
  0.0 39.3 jit_solution(1451046482651170052)
XLA Ops:
  0.0 0.0 copy-start.8
  0.0 0.7 %copy-done.8 = s32[4096]{0:T(1024)S(1)} copy-done((s32[4096]{0:T(1024)S(1)}, s32[4096]{0:T(1024)}, u32[]{:S(2)}) %copy-start.8) | copy-done | bytes 16408
  0.7 0.8 %fusion.1.ids_ref = s32[3,512]{1,0:T(4,128)S(1)} fusion(s32[]{:T(128)S(6)} %select_n.3, s32[1,4096]{1,0:T(1,128)S(1)} %bitcast.7, s32[1,4096]{1,0:T(1,128)} %bitcast.8, s32[1,4096]{1,0:T(1,128)} %bitcast.9), kind=kLoop, calls=%fused_computation.4 | loop fusion | flops 3072 | bytes 55300 | tf_op jit(solution)/shard_map/stack | solution.py:419
  1.5 0.0 copy-start.3
  1.5 0.0 copy-start.4
  1.5 0.0 copy-start.5
  1.5 0.0 copy-start.6
  1.5 0.0 copy-start.7
  1.6 0.6 %copy-done.3 = s32[8,8]{1,0:T(8,128)S(1)} copy-done((s32[8,8]{1,0:T(8,128)S(1)}, s32[8,8]{1,0:T(8,128)}, u32[]{:S(2)}) %copy-start.3) | copy-done | bytes 280
  2.2 0.0 copy-done.4
  2.2 0.0 copy-done.5
  2.2 0.0 copy-done.6
  2.2 0.0 copy-done.7
  2.2 0.0 copy-start.1
  2.2 0.9 %copy-done.1 = f32[3,8192]{1,0:T(4,128)S(1)} copy-done((f32[3,8192]{1,0:T(4,128)S(1)}, f32[3,8192]{1,0:T(4,128)}, u32[]{:S(2)}) %copy-start.1) | copy-done | bytes 98328
  3.1 0.0 copy-start.2
  3.1 0.9 %copy-done.2 = f32[1,32,2,512]{3,2,1,0:T(2,128)S(1)} copy-done((f32[1,32,2,512]{3,2,1,0:T(2,128)S(1)}, f32[1,32,2,512]{3,2,1,0:T(2,128)}, u32[]{:S(2)}) %copy-start.2) | copy-done | bytes 131096
  4.1 2.9 %prepare.1 = (f32[3,128,128]{2,1,0:T(8,128)S(1)}, f32[128,8,128]{2,1,0:T(8,128)S(1)}, f32[5,8,128]{2,1,0:T(8,128)S(1)}, f32[8,3,1024]{2,1,0:T(4,128)S(1)}, f32[4...) custom-call(f32[3,8192]{1,0:T(4,128)S(1)} %copy-done.1, f32[1,32]{1,0:T(1,128)S(1)} %bitcast.5, ...), custom_call_target="tpu_custom_call" | custom-call | tf_op jit(solution)/shard_map/prepare/pallas_call | solution.py:426
  6.9 0.0 copy-start
  6.9 30.8 %predict.1.piece_ref = f32[8,2,8,1024]{3,2,1,0:T(8,128)S(1)} custom-call(f32[3,128,128]{2,1,0:T(8,128)S(1)} %get-tuple-element.13.sky_ref, f32[128,8,128]{2,1,0:T(8,128)S(1)} %get-tuple-element.14.wide_ref, f32[5,8,128]{2,1,0:T(8,128)S(1)} %get-tuple-element.15.base_ref, f32[8,3,1024]{2,1,0:T(4,128)S(1)} %get-tuple-element.16.order_ref, ...), custom_call_target="tpu_custom_call" | custom-call | tf_op jit(solution)/shard_map/predict/pallas_call | solution.py:455
  37.8 0.0 copy-done
  37.8 1.5 %place.1 = f32[8,2,3840]{2,1,0:T(2,128)} custom-call(s32[1,128]{1,0:T(1,128)S(1)} %get-tuple-element.12.start_ref, f32[8,2,8,1024]{3,2,1,0:T(8,128)S(1)} %predict.1.piece_ref, f32[8,2,3840]{2,1,0:T(2,128)S(1)} %copy-done), custom_call_target="tpu_custom_call" | custom-call | tf_op jit(solution)/shard_map/place/pallas_call | solution.py:476
  (1 shorter events, 0.0 us)
Async XLA Ops:
  0.0 0.7 %copy-start.8 = (s32[4096]{0:T(1024)S(1)}, s32[4096]{0:T(1024)}, u32[]{:S(2)}) copy-start(s32[4096]{0:T(1024)} %param.20) | copy-start | bytes 49156
  1.5 0.7 %copy-start.3 = (s32[8,8]{1,0:T(8,128)S(1)}, s32[8,8]{1,0:T(8,128)}, u32[]{:S(2)}) copy-start(s32[8,8]{1,0:T(8,128)} %plan_smem.1) | copy-start | bytes 772
  1.5 0.7 %copy-start.4 = (f32[32,128]{1,0:T(8,128)S(1)}, f32[32,128]{1,0:T(8,128)}, u32[]{:S(2)}) copy-start(f32[32,128]{1,0:T(8,128)} %flux_ref.1) | copy-start | bytes 49156
  1.5 0.7 %copy-start.5 = (f32[2,128]{1,0:T(2,128)S(1)}, f32[2,128]{1,0:T(2,128)}, u32[]{:S(2)}) copy-start(f32[2,128]{1,0:T(2,128)} %offs_ref.1) | copy-start | bytes 3076
  1.5 0.7 %copy-start.6 = (f32[32]{0:T(128)S(1)}, f32[32]{0:T(128)}, u32[]{:S(2)}) copy-start(f32[32]{0:T(128)} %param.13) | copy-start | bytes 388
  1.5 0.7 %copy-start.7 = (s32[128]{0:T(128)S(1)}, s32[128]{0:T(128)}, u32[]{:S(2)}) copy-start(s32[128]{0:T(128)} %param.16) | copy-start | bytes 1540
  2.2 0.9 %copy-start.1 = (f32[3,8192]{1,0:T(4,128)S(1)}, f32[3,8192]{1,0:T(4,128)}, u32[]{:S(2)}) copy-start(f32[3,8192]{1,0:T(4,128)} %uvw_ref.1) | copy-start | bytes 294916
  3.1 0.9 %copy-start.2 = (f32[1,32,2,512]{3,2,1,0:T(2,128)S(1)}, f32[1,32,2,512]{3,2,1,0:T(2,128)}, u32[]{:S(2)}) copy-start(f32[1,32,2,512]{3,2,1,0:T(2,128)} %gain_ref.1) | copy-start | bytes 393220
  6.9 30.8 %copy-start = (f32[8,2,3840]{2,1,0:T(2,128)S(1)}, f32[8,2,3840]{2,1,0:T(2,128)}, u32[]{:S(2)}) copy-start(f32[8,2,3840]{2,1,0:T(2,128)} %observed_ref.1) | copy-start | bytes 737284

commit v2 on v1

--- a/solution.py
+++ b/solution.py
@@ -10,6 +10,7 @@
 
 LANES = 128
 UNROLL = 32
+EARLY = 3
 MESH = pl.DeviceIdType.MESH
 HIGH = lax.Precision.HIGHEST
 NT = (((1,), (1,)), ((), ()))
@@ -21,6 +22,11 @@
     return lax.broadcasted_iota(jnp.int32, shape, axis)
 
 
+def flip(a, b, size):
+    bits = range(int(math.log2(size)))
+    return sum(((a // 2**i + b // 2**i) % 2) * 2**i for i in bits)
+
+
 def take(values, index):
     return jnp.take_along_axis(values, index, axis=1, mode="promise_in_bounds")
 
@@ -29,16 +35,10 @@
     groups,
     owners,
     time,
-    uvw_ref,
-    freq_ref,
-    offs_ref,
-    flux_ref,
-    group_ref,
-    gain_ref,
-    ids_ref,
-    exps_ref,
-    plan_ref,
-    plan_smem,
+    *refs,
+):
+    inputs = refs[:11]
+    (
     sky_ref,
     wide_ref,
     base_ref,
@@ -47,13 +47,37 @@
     mask_ref,
     start_ref,
     table_ref,
-):
+    uvw_ref,
+    freq_ref,
+    offs_ref,
+    flux_ref,
+    group_ref,
+    gain_ref,
+    first_ref,
+    second_ref,
+    exps_ref,
+    plan_ref,
+    plan_smem,
+    sem,
+    ) = refs[11:]
     d = lax.axis_index("dir")
     p = lax.axis_index("bl")
     cl = wide_ref.shape[1]
     sources = offs_ref.shape[1]
     per_group = sources // groups
-    bl_dev = ids_ref.shape[1]
+    bl_dev = first_ref.shape[1]
+    own = pl.ds(pl.multiple_of(p * bl_dev, bl_dev), bl_dev)
+    held = refs[19:30]
+    copies = {}
+    for index in (4, 2, 3, 1, 9, 10, 0, 5, 6, 7, 8):
+        source = inputs[index].at[:, own] if index in (6, 7) else inputs[index]
+        copies[index] = pltpu.make_async_copy(source, held[index], sem.at[index])
+        copies[index].start()
+
+    def arrive(*indices):
+        for index in indices:
+            copies[index].wait()
+
     block_len = bl_dev // owners
     slots = block_len * time
     block_tiles = slots // LANES
@@ -61,17 +85,7 @@
     log_time = int(math.log2(time))
     chunks = bl_dev // LANES
 
-    for k in range(owners):
-        order_ref[plan_smem[p, k]] = uvw_ref[:, k * slots : (k + 1) * slots]
-    plan = plan_ref[...].astype(jnp.float32)
-    own_plan = jnp.sum(
-        jnp.where(iota((owners, owners), 0) == p, plan, 0.0), axis=0, keepdims=True
-    )
-    held_by = jnp.abs(own_plan - iota((owners, owners), 0).astype(jnp.float32)) < 0.5
-    block_of = jnp.sum(
-        jnp.where(held_by, iota((owners, owners), 1).astype(jnp.float32), 0.0), axis=1, keepdims=True
-    )
-
+    arrive(4, 2, 3, 1)
     member_row = group_ref[...].astype(jnp.float32)
     eye = (iota((sources, sources), 0) == iota((sources, sources), 1)).astype(jnp.float32)
     member_col = lax.dot_general(eye, member_row, NT, precision=HIGH)
@@ -98,6 +112,19 @@
     freq = jnp.sum(channel * freq_ref[...], axis=1, keepdims=True)
     base_ref[groups] = jnp.broadcast_to(freq, (cl, LANES))
 
+    arrive(9, 10, 0)
+    for k in range(owners):
+        order_ref[plan_smem[p, k]] = uvw_ref[:, k * slots : (k + 1) * slots]
+    plan = plan_ref[...].astype(jnp.float32)
+    own_plan = jnp.sum(
+        jnp.where(iota((owners, owners), 0) == p, plan, 0.0), axis=0, keepdims=True
+    )
+    held_by = jnp.abs(own_plan - iota((owners, owners), 0).astype(jnp.float32)) < 0.5
+    block_of = jnp.sum(
+        jnp.where(held_by, iota((owners, owners), 1).astype(jnp.float32), 0.0), axis=1, keepdims=True
+    )
+
+    arrive(5, 6, 7, 8)
     lane = iota((owners, LANES), 1)
     row = iota((owners, LANES), 0)
     station_total = gain_ref.shape[3]
@@ -114,7 +141,7 @@
         for which in range(2):
             ids = jnp.zeros((cl, LANES), jnp.int32)
             for part in range(chunks):
-                table = ids_ref[which : which + 1, part * LANES : (part + 1) * LANES]
+                table = (first_ref, second_ref)[which][:, part * LANES : (part + 1) * LANES]
                 table = jnp.broadcast_to(table, (cl, LANES))
                 ids = jnp.where((source >> 7) == part, take(table, source & (LANES - 1)), ids)
             low, high = ids & (LANES - 1), ids >> 7
@@ -133,7 +160,10 @@
             pair_ref[g, 0, :, lanes] = ar * br + ai * bi
             pair_ref[g, 1, :, lanes] = ai * br - ar * bi
 
-    rows_all = jnp.right_shift(jnp.full(exps_ref.shape, time, jnp.int32), exps_ref[...])
+    exps_all = jnp.concatenate(
+        [exps_ref[:, i * bl_dev : (i + 1) * bl_dev] for i in range(owners)], axis=0
+    )
+    rows_all = jnp.right_shift(jnp.full(exps_all.shape, time, jnp.int32), exps_all)
     rows_all = rows_all.astype(jnp.float32)
     to_owner = jnp.zeros((owners, 1), jnp.float32)
     for k in range(owners):
@@ -147,7 +177,8 @@
         source = (block_of + 0.5).astype(jnp.int32) * block_len + t * per_tile + lane // time
         found = jnp.zeros((owners, LANES), jnp.int32)
         for part in range(chunks):
-            table = ids_ref[2:3, part * LANES : (part + 1) * LANES]
+            begin = pl.multiple_of(p * bl_dev + part * LANES, LANES)
+            table = exps_ref[:, pl.ds(begin, LANES)]
             table = jnp.broadcast_to(table, (owners, LANES))
             if owners > 8:
                 got = jnp.concatenate(
@@ -229,6 +260,9 @@
                 barrier, inc=1, device_id={axis: lax.rem(me + step, size)}, device_id_type=MESH
             )
 
+    def owner_of(turn):
+        return flip(p, owners - 1 - turn, owners)
+
     def gain_copy(step):
         other = lax.rem(d + step, groups)
         return pltpu.make_async_remote_copy(
@@ -246,7 +280,7 @@
             dst_ref=piece_ref.at[p],
             send_sem=piece_send.at[step],
             recv_sem=piece_recv.at[step],
-            device_id={"bl": lax.rem(p + 1 + step, owners)},
+            device_id={"bl": owner_of(step)},
             device_id_type=MESH,
         )
 
@@ -256,10 +290,7 @@
     lane = iota((cl, LANES), 1)
     steps = block_tiles // tiles
 
-    def owner_of(turn):
-        return lax.rem(p + 1 + turn, owners)
-
-    def add_sources(owner, step, keep_ref):
+    def add_sources(owner, step, keep_ref, sent=()):
         for t in range(tiles):
             ln = pl.ds(pl.multiple_of((step * tiles + t) * LANES, LANES), LANES)
             u = order_ref[owner, 0:1, ln]
@@ -288,6 +319,9 @@
             for t in range(tiles):
                 keep_ref[step * tiles + t, 2 * g] = K0 * flux_sum[g] + K1 * acc[2 * t]
                 keep_ref[step * tiles + t, 2 * g + 1] = -K2 * acc[2 * t + 1]
+            if g == groups // 2 - 1:
+                for done in sent:
+                    piece_copy(done).start()
 
     def finish(turn, keep_ref):
         owner = owner_of(turn)
@@ -339,27 +373,30 @@
         add_sources(owner_of(turn), lax.rem(index, steps), early_ref.at[turn])
         return carry
 
-    lax.fori_loop(0, 2 * steps, early, 0)
+    lax.fori_loop(0, EARLY * steps, early, 0)
     for step in range(1, groups):
         gain_copy(step).wait()
-    for step in range(steps):
-        done = [turn for turn in range(2) if min(turn, steps - 1) == step]
-        for turn in done:
-            send(turn, finish(turn, early_ref.at[turn]))
-        add_sources(owner_of(2), step, sum_ref)
-        for turn in done:
-            piece_copy(turn).start()
+    turn, ready, quota = EARLY, 0, 2 // steps if steps < 2 else 1
+    kept = {turn: early_ref.at[turn] for turn in range(EARLY)}
+    while ready < turn - 1:
+        last = ready + quota * steps >= turn
+        kept[turn] = sum_ref if last else early_ref.at[turn]
+        for step in range(steps):
+            now = list(range(ready, min(ready + quota, turn)))
+            for done in now:
+                send(done, finish(done, kept[done]))
+            add_sources(owner_of(turn), step, kept[turn], now)
+            ready += len(now)
+        turn += 1
 
     def block_body(turn, carry):
-        for step in range(steps):
-            if step == 0:
-                send(turn - 1, finish(turn - 1, sum_ref))
+        send(turn - 1, finish(turn - 1, sum_ref))
+        add_sources(owner_of(turn), 0, sum_ref, [turn - 1])
+        for step in range(1, steps):
             add_sources(owner_of(turn), step, sum_ref)
-            if step == 0:
-                piece_copy(turn - 1).start()
         return carry
 
-    lax.fori_loop(3, owners, block_body, 0)
+    lax.fori_loop(turn, owners, block_body, 0)
     done = finish(owners - 1, sum_ref)
     for z in range(2):
         piece_ref[p, z] = done[z]
@@ -416,8 +453,6 @@
     slots = rows // owners
     tiles = slots // LANES
     sources = source_group.shape[0]
-    ids = jnp.stack([station_first, station_second, average_exponent])
-    ids = lax.dynamic_slice_in_dim(ids, lax.axis_index("bl") * bl_dev, bl_dev, 1)
     vmem = pl.BlockSpec(memory_space=pltpu.VMEM)
     smem = pl.BlockSpec(memory_space=pltpu.SMEM)
     masks = int(math.log2(time)) + int(math.log2(slots)) + 2
@@ -434,22 +469,42 @@
             shape((masks, tiles, owners, LANES), f32),
             shape((1, LANES), jnp.int32),
         ),
-        in_specs=[vmem] * 9 + [smem],
+        in_specs=[pl.BlockSpec(memory_space=pltpu.HBM)] * 11,
         out_specs=(vmem,) * 7,
-        scratch_shapes=[pltpu.VMEM((groups, 2, cl, direction_gain.shape[3]), f32)],
+        scratch_shapes=[
+            pltpu.VMEM((groups, 2, cl, direction_gain.shape[3]), f32),
+            pltpu.VMEM(baseline_uvw_rows.shape, f32),
+            pltpu.VMEM((1, frequencies.shape[0]), f32),
+            pltpu.VMEM(source_offset.shape, f32),
+            pltpu.VMEM(source_flux.shape, f32),
+            pltpu.VMEM((1, sources), jnp.int32),
+            pltpu.VMEM(direction_gain.shape, f32),
+            pltpu.VMEM((1, bl_dev), jnp.int32),
+            pltpu.VMEM((1, bl_dev), jnp.int32),
+            pltpu.VMEM((1, average_exponent.shape[0]), jnp.int32),
+            pltpu.VMEM(owner_plan.shape, jnp.int32),
+            pltpu.SMEM(owner_plan.shape, jnp.int32),
+            pltpu.SemaphoreType.DMA((11,)),
+        ],
         compiler_params=pltpu.CompilerParams(vmem_limit_bytes=32 << 20),
         name="prepare",
     )(
-        baseline_uvw_rows,
-        frequencies.reshape(1, -1),
-        source_offset,
-        source_flux,
-        source_group.reshape(1, -1),
-        direction_gain,
-        ids,
-        average_exponent.reshape(owners, bl_dev),
-        owner_plan,
-        owner_plan,
+        *[
+            pltpu.with_memory_space_constraint(array, pltpu.HBM)
+            for array in (
+                baseline_uvw_rows,
+                frequencies.reshape(1, -1),
+                source_offset,
+                source_flux,
+                source_group.reshape(1, -1),
+                direction_gain,
+                station_first.reshape(1, -1),
+                station_second.reshape(1, -1),
+                average_exponent.reshape(1, -1),
+                owner_plan,
+                owner_plan,
+            )
+        ]
     )
     dma = pltpu.SemaphoreType.DMA
     pieces = pl.pallas_call(
@@ -460,7 +515,7 @@
         scratch_shapes=[
             pltpu.VMEM((min(4, tiles), sources, LANES), f32),
             pltpu.VMEM((tiles, 2 * groups, cl, LANES), f32),
-            pltpu.VMEM((2, tiles, 2 * groups, cl, LANES), f32),
+            pltpu.VMEM((EARLY + 1, tiles, 2 * groups, cl, LANES), f32),
             pltpu.VMEM((owners - 1, 2, cl, slots), f32),
             pltpu.VMEM((groups, 2, cl, bl_dev), f32),
             dma((groups - 1,)),

time: 39.6 us -> 34 us (0.86)
  the two profiles are of different devices: /device:TPU:1 before, /device:TPU:0 now
where the time goes in v2:
time: 34 us; the launch traced here: 33.9 us
  Pallas kernels  33.8 us (99%)
    pallas_call x1, Pallas kernels, on_device(): pl.pallas_call(functools.partial(predict_kernel, groups, owners, time, mi...  28.8 us
    pallas_call x1, Pallas kernels, on_device(): pl.pallas_call(functools.partial(prepare_kernel, groups, owners, time), o...  3.49 us
    pallas_call x1, Pallas kernels, on_device(): pl.pallas_call(place_kernel, out_shape=jax.ShapeDtypeStruct(observed.shap...  1.51 us

profile of v2, /device:TPU:0, one launch (start us, length us, event | category | flops | bytes accessed | tf_op | source)
XLA Modules:
  0.0 33.9 jit_solution(3311001951427821813)
XLA Ops:
  0.0 3.5 %prepare.1 = (f32[3,128,128]{2,1,0:T(8,128)S(1)}, f32[128,8,128]{2,1,0:T(8,128)S(1)}, f32[5,8,128]{2,1,0:T(8,128)S(1)}, f32[8,3,1024]{2,1,0:T(4,128)S(1)}, f32[4...) custom-call(f32[3,8192]{1,0:T(4,128)} %refs_0_.1, f32[1,32]{1,0:T(1,128)} %bitcast.8, ...), custom_call_target="tpu_custom_call" | custom-call | tf_op jit(solution)/shard_map/prepare/pallas_call | solution.py:461
  3.5 0.0 copy-start
  3.5 28.8 %predict.1.piece_ref = f32[8,2,8,1024]{3,2,1,0:T(8,128)S(1)} custom-call(f32[3,128,128]{2,1,0:T(8,128)S(1)} %get-tuple-element.13.sky_ref, f32[128,8,128]{2,1,0:T(8,128)S(1)} %get-tuple-element.14.wide_ref, f32[5,8,128]{2,1,0:T(8,128)S(1)} %get-tuple-element.15.base_ref, f32[8,3,1024]{2,1,0:T(4,128)S(1)} %get-tuple-element.16.order_ref, ...), custom_call_target="tpu_custom_call" | custom-call | tf_op jit(solution)/shard_map/predict/pallas_call | solution.py:510
  32.4 0.0 copy-done
  32.4 1.5 %place.1 = f32[8,2,3840]{2,1,0:T(2,128)} custom-call(s32[1,128]{1,0:T(1,128)S(1)} %get-tuple-element.12.start_ref, f32[8,2,8,1024]{3,2,1,0:T(8,128)S(1)} %predict.1.piece_ref, f32[8,2,3840]{2,1,0:T(2,128)S(1)} %copy-done), custom_call_target="tpu_custom_call" | custom-call | tf_op jit(solution)/shard_map/place/pallas_call | solution.py:531
Async XLA Ops:
  3.5 28.9 %copy-start = (f32[8,2,3840]{2,1,0:T(2,128)S(1)}, f32[8,2,3840]{2,1,0:T(2,128)}, u32[]{:S(2)}) copy-start(f32[8,2,3840]{2,1,0:T(2,128)} %observed_ref.1) | copy-start | bytes 737284

commit v3 on v2

--- a/solution.py
+++ b/solution.py
@@ -10,7 +10,8 @@
 
 LANES = 128
 UNROLL = 32
-EARLY = 3
+EARLY = 4
+START = 3
 MESH = pl.DeviceIdType.MESH
 HIGH = lax.Precision.HIGHEST
 NT = (((1,), (1,)), ((), ()))
@@ -29,6 +30,13 @@
 
 def take(values, index):
     return jnp.take_along_axis(values, index, axis=1, mode="promise_in_bounds")
+
+
+def thirds(value):
+    high = value.astype(jnp.bfloat16).astype(jnp.float32)
+    rest = value - high
+    mid = rest.astype(jnp.bfloat16).astype(jnp.float32)
+    return high, mid, rest - mid
 
 
 def prepare_kernel(
@@ -47,6 +55,7 @@
     mask_ref,
     start_ref,
     table_ref,
+    spread_ref,
     uvw_ref,
     freq_ref,
     offs_ref,
@@ -67,7 +76,7 @@
     per_group = sources // groups
     bl_dev = first_ref.shape[1]
     own = pl.ds(pl.multiple_of(p * bl_dev, bl_dev), bl_dev)
-    held = refs[19:30]
+    held = refs[20:31]
     copies = {}
     for index in (4, 2, 3, 1, 9, 10, 0, 5, 6, 7, 8):
         source = inputs[index].at[:, own] if index in (6, 7) else inputs[index]
@@ -97,9 +106,24 @@
     offs = lax.dot_general(pick, offs_ref[...], NT, precision=HIGH)
     east, north = offs[:, 0:1], offs[:, 1:2]
     depth = jnp.sqrt(1.0 - east * east - north * north) - 1.0
-    sky_ref[0] = jnp.broadcast_to(east, sky_ref.shape[1:])
-    sky_ref[1] = jnp.broadcast_to(north, sky_ref.shape[1:])
-    sky_ref[2] = jnp.broadcast_to(depth, sky_ref.shape[1:])
+    depth_of = sky_ref.shape[1]
+    kind = iota((sources, depth_of), 1) % 8
+    spread_ref[...] = jnp.where(
+        kind == 0, east, jnp.where(kind == 1, north, jnp.where(kind == 2, depth, 0.0))
+    )
+    high_rows = sky_ref.shape[0] // sources
+    turn_channel = iota((high_rows, flux_ref.shape[0]), 1) == d * cl + iota((high_rows, flux_ref.shape[0]), 0)
+    turn_freq = jnp.sum(turn_channel.astype(jnp.float32) * freq_ref[...], axis=1, keepdims=True)
+    turn_freq = jnp.broadcast_to(turn_freq, (high_rows, depth_of))
+    term = iota((high_rows, depth_of), 1) // 8
+    pair_rows = max(1, 16 // high_rows)
+    for k in range(0, sources, pair_rows):
+        rows = []
+        for i in range(pair_rows):
+            high, mid, low = thirds(turn_freq * spread_ref[pl.ds(k + i, high_rows, stride=0), :])
+            rows.append(jnp.where((term == 2) | (term == 3), mid, jnp.where(term == 5, low, high)))
+        rows = jnp.concatenate(rows, axis=0).astype(jnp.bfloat16)
+        sky_ref[k * high_rows : (k + pair_rows) * high_rows, :] = rows
     channel = iota((cl, flux_ref.shape[0]), 1) == d * cl + iota((cl, flux_ref.shape[0]), 0)
     channel = channel.astype(jnp.float32)
     own_flux = jnp.dot(channel, flux_ref[...], precision=HIGH)
@@ -109,12 +133,14 @@
     for g in range(groups):
         part = jnp.sum(flux[:, g * per_group : (g + 1) * per_group], axis=1, keepdims=True)
         base_ref[g] = jnp.broadcast_to(part, (cl, LANES))
-    freq = jnp.sum(channel * freq_ref[...], axis=1, keepdims=True)
-    base_ref[groups] = jnp.broadcast_to(freq, (cl, LANES))
 
     arrive(9, 10, 0)
     for k in range(owners):
-        order_ref[plan_smem[p, k]] = uvw_ref[:, k * slots : (k + 1) * slots]
+        rows = uvw_ref[:, k * slots : (k + 1) * slots]
+        rows = jnp.concatenate([rows, jnp.zeros((8 - rows.shape[0], slots), jnp.float32)], axis=0)
+        high, mid, low = thirds(rows)
+        rows = jnp.concatenate([high, mid, high, mid, low, high], axis=0)
+        order_ref[plan_smem[p, k]] = rows.astype(jnp.bfloat16)
     plan = plan_ref[...].astype(jnp.float32)
     own_plan = jnp.sum(
         jnp.where(iota((owners, owners), 0) == p, plan, 0.0), axis=0, keepdims=True
@@ -232,9 +258,8 @@
     pair_ref,
     mask_ref,
     piece_ref,
-    q_ref,
-    sum_ref,
-    early_ref,
+    turns_ref,
+    kept_ref,
     send_ref,
     gather_ref,
     gain_send,
@@ -285,26 +310,33 @@
         )
 
     gather_ref[d] = pair_ref[d]
-    freq = base_ref[groups]
     flux_sum = [base_ref[g] for g in range(groups)]
     lane = iota((cl, LANES), 1)
     steps = block_tiles // tiles
 
-    def add_sources(owner, step, keep_ref, sent=()):
-        for t in range(tiles):
-            ln = pl.ds(pl.multiple_of((step * tiles + t) * LANES, LANES), LANES)
-            u = order_ref[owner, 0:1, ln]
-            v = order_ref[owner, 1:2, ln]
-            w = order_ref[owner, 2:3, ln]
-            q_ref[t] = sky_ref[0] * u + sky_ref[1] * v + sky_ref[2] * w
+    def fill(turn, step, g):
+        ln = pl.ds(pl.multiple_of(step * tiles * LANES, LANES), tiles * LANES)
+        rows = per_group * turns_ref.shape[2]
+        turns = jnp.dot(
+            sky_ref[g * rows : (g + 1) * rows, :],
+            order_ref[owner_of(turn), :, ln],
+            preferred_element_type=jnp.float32,
+        )
+        turns_ref[g] = turns.reshape(turns_ref.shape[1:])
+
+    def add_sources(turn, step, sent=()):
         for g in range(groups):
+            if g + 1 < groups:
+                fill(turn, step, g + 1)
+            else:
+                fill(lax.rem(turn + (step + 1) // steps, owners), lax.rem(step + 1, steps), 0)
 
             def source(i, acc):
                 acc = list(acc)
                 index = g * per_group + i
                 amount = wide_ref[index]
                 for t in range(tiles):
-                    turns = freq * q_ref[t, pl.ds(index, cl, stride=0), :]
+                    turns = turns_ref[g, i, 0:cl, t * LANES : (t + 1) * LANES]
                     x = turns - jnp.round(turns)
                     z = x * x
                     m = (z + P0) * z
@@ -317,13 +349,13 @@
             acc = tuple(jnp.zeros((cl, LANES), jnp.float32) for _ in range(2 * tiles))
             acc = lax.fori_loop(0, per_group, source, acc, unroll=UNROLL)
             for t in range(tiles):
-                keep_ref[step * tiles + t, 2 * g] = K0 * flux_sum[g] + K1 * acc[2 * t]
-                keep_ref[step * tiles + t, 2 * g + 1] = -K2 * acc[2 * t + 1]
+                kept_ref[turn, step * tiles + t, 2 * g] = K0 * flux_sum[g] + K1 * acc[2 * t]
+                kept_ref[turn, step * tiles + t, 2 * g + 1] = -K2 * acc[2 * t + 1]
             if g == groups // 2 - 1:
                 for done in sent:
                     piece_copy(done).start()
 
-    def finish(turn, keep_ref):
+    def finish(turn):
         owner = owner_of(turn)
         model = ([], [])
         for t in range(block_tiles):
@@ -335,7 +367,7 @@
             for g in range(groups):
                 gr = take(gather_ref[g, 0, :, pl.ds(chunk, LANES)], index)
                 gi = take(gather_ref[g, 1, :, pl.ds(chunk, LANES)], index)
-                real, imag = keep_ref[t, 2 * g], keep_ref[t, 2 * g + 1]
+                real, imag = kept_ref[turn, t, 2 * g], kept_ref[turn, t, 2 * g + 1]
                 model_r = model_r + (real * gr - imag * gi)
                 model_i = model_i + (real * gi + imag * gr)
             model[0].append(model_r)
@@ -362,42 +394,41 @@
             send_ref[turn, z] = done[z]
 
     def early(index, carry):
-        turn = index // steps
-
-        @pl.when(index == steps)
+        @pl.when(index == START)
         def _():
             pl.semaphore_wait(barrier, groups - 1 + owners - 1)
             for step in range(1, groups):
                 gain_copy(step).start()
 
-        add_sources(owner_of(turn), lax.rem(index, steps), early_ref.at[turn])
+        add_sources(index // steps, lax.rem(index, steps))
         return carry
 
+    fill(0, 0, 0)
     lax.fori_loop(0, EARLY * steps, early, 0)
     for step in range(1, groups):
         gain_copy(step).wait()
-    turn, ready, quota = EARLY, 0, 2 // steps if steps < 2 else 1
-    kept = {turn: early_ref.at[turn] for turn in range(EARLY)}
-    while ready < turn - 1:
-        last = ready + quota * steps >= turn
-        kept[turn] = sum_ref if last else early_ref.at[turn]
+
+    def catch_up(index, carry):
         for step in range(steps):
-            now = list(range(ready, min(ready + quota, turn)))
+            first = 2 * index + (step if steps > 1 else 0)
+            now = [first] if 0 < steps - 1 else [first, first + 1]
+            now = now if step < 2 else []
             for done in now:
-                send(done, finish(done, kept[done]))
-            add_sources(owner_of(turn), step, kept[turn], now)
-            ready += len(now)
-        turn += 1
+                send(done, finish(done))
+            add_sources(EARLY + index, step, now)
+        return carry
+
+    lax.fori_loop(0, EARLY - 1, catch_up, 0)
 
     def block_body(turn, carry):
-        send(turn - 1, finish(turn - 1, sum_ref))
-        add_sources(owner_of(turn), 0, sum_ref, [turn - 1])
+        send(turn - 1, finish(turn - 1))
+        add_sources(turn, 0, [turn - 1])
         for step in range(1, steps):
-            add_sources(owner_of(turn), step, sum_ref)
+            add_sources(turn, step)
         return carry
 
-    lax.fori_loop(turn, owners, block_body, 0)
-    done = finish(owners - 1, sum_ref)
+    lax.fori_loop(2 * EARLY - 1, owners, block_body, 0)
+    done = finish(owners - 1)
     for z in range(2):
         piece_ref[p, z] = done[z]
     for step in range(owners - 1):
@@ -456,15 +487,16 @@
     vmem = pl.BlockSpec(memory_space=pltpu.VMEM)
     smem = pl.BlockSpec(memory_space=pltpu.SMEM)
     masks = int(math.log2(time)) + int(math.log2(slots)) + 2
+    rows_per = max(8, cl)
     f32 = jnp.float32
     shape = jax.ShapeDtypeStruct
     *prepared, starts = pl.pallas_call(
         functools.partial(prepare_kernel, groups, owners, time),
         out_shape=(
-            shape((3, sources, LANES), f32),
+            shape((sources * rows_per, 48), jnp.bfloat16),
             shape((sources, cl, LANES), f32),
-            shape((groups + 1, cl, LANES), f32),
-            shape((owners, 3, slots), f32),
+            shape((groups, cl, LANES), f32),
+            shape((owners, 48, slots), jnp.bfloat16),
             shape((groups, 2, cl, bl_dev), f32),
             shape((masks, tiles, owners, LANES), f32),
             shape((1, LANES), jnp.int32),
@@ -473,6 +505,7 @@
         out_specs=(vmem,) * 7,
         scratch_shapes=[
             pltpu.VMEM((groups, 2, cl, direction_gain.shape[3]), f32),
+            pltpu.VMEM((sources, 48), f32),
             pltpu.VMEM(baseline_uvw_rows.shape, f32),
             pltpu.VMEM((1, frequencies.shape[0]), f32),
             pltpu.VMEM(source_offset.shape, f32),
@@ -513,9 +546,8 @@
         in_specs=[vmem] * 6,
         out_specs=vmem,
         scratch_shapes=[
-            pltpu.VMEM((min(4, tiles), sources, LANES), f32),
-            pltpu.VMEM((tiles, 2 * groups, cl, LANES), f32),
-            pltpu.VMEM((EARLY + 1, tiles, 2 * groups, cl, LANES), f32),
+            pltpu.VMEM((groups, sources // groups, rows_per, min(4, tiles) * LANES), f32),
+            pltpu.VMEM((owners, tiles, 2 * groups, cl, LANES), f32),
             pltpu.VMEM((owners - 1, 2, cl, slots), f32),
             pltpu.VMEM((groups, 2, cl, bl_dev), f32),
             dma((groups - 1,)),

time: 34 us -> 31.9 us (0.938)
  Pallas kernels: 33.8 us -> 31.7 us
    pallas_call x1, Pallas kernels: 28.8 us -> 26.6 us  [on_device(): pl.pallas_call(functools.partial(predict_kernel, groups, owners, time, mi...]
where the time goes in v3:
time: 31.9 us; the launch traced here: 31.7 us
  Pallas kernels  31.7 us (99%)
    pallas_call x1, Pallas kernels, on_device(): pl.pallas_call(functools.partial(predict_kernel, groups, owners, time, mi...  26.6 us
    pallas_call x1, Pallas kernels, on_device(): pl.pallas_call(functools.partial(prepare_kernel, groups, owners, time), o...  3.6 us
    pallas_call x1, Pallas kernels, on_device(): pl.pallas_call(place_kernel, out_shape=jax.ShapeDtypeStruct(observed.shap...  1.51 us

profile of v3, /device:TPU:0, one launch (start us, length us, event | category | flops | bytes accessed | tf_op | source)
XLA Modules:
  0.0 31.7 jit_solution(13346846906082270527)
XLA Ops:
  0.0 3.6 %prepare.1 = (bf16[1024,48]{1,0:T(8,128)(2,1)S(1)}, f32[128,8,128]{2,1,0:T(8,128)S(1)}, f32[4,8,128]{2,1,0:T(8,128)S(1)}, bf16[8,48,1024]{2,1,0:T(8,128)(2,1)S(1...) custom-call(f32[3,8192]{1,0:T(4,128)} %refs_0_.1, f32[1,32]{1,0:T(1,128)} %bitcast.8, ...), custom_call_target="tpu_custom_call" | custom-call | tf_op jit(solution)/shard_map/prepare/pallas_call | solution.py:493
  3.6 0.0 copy-start
  3.6 26.6 %predict.1.piece_ref = f32[8,2,8,1024]{3,2,1,0:T(8,128)S(1)} custom-call(bf16[1024,48]{1,0:T(8,128)(2,1)S(1)} %get-tuple-element.13.sky_ref, f32[128,8,128]{2,1,0:T(8,128)S(1)} %get-tuple-element.14.wide_ref, f32[4,8,128]{2,1,0:T(8,128)S(1)} %get-tuple-element.15.base_ref, bf16[8,48,1024]{2,1,0:T(8,128)(2,1)S(1)} %get-tuple-element.16.order_ref, ...), custom_call_target="tpu_custom_call" | custom-call | tf_op jit(solution)/shard_map/predict/pallas_call | solution.py:543
  30.2 0.0 copy-done
  30.2 1.5 %place.1 = f32[8,2,3840]{2,1,0:T(2,128)} custom-call(s32[1,128]{1,0:T(1,128)S(1)} %get-tuple-element.12.start_ref, f32[8,2,8,1024]{3,2,1,0:T(8,128)S(1)} %predict.1.piece_ref, f32[8,2,3840]{2,1,0:T(2,128)S(1)} %copy-done), custom_call_target="tpu_custom_call" | custom-call | tf_op jit(solution)/shard_map/place/pallas_call | solution.py:563
Async XLA Ops:
  3.6 26.6 %copy-start = (f32[8,2,3840]{2,1,0:T(2,128)S(1)}, f32[8,2,3840]{2,1,0:T(2,128)}, u32[]{:S(2)}) copy-start(f32[8,2,3840]{2,1,0:T(2,128)} %observed_ref.1) | copy-start | bytes 737284
